TPU v7x, 32 devices: a whole 2x2x4 slice. The times are simulated.
32 devices in a mesh: dom: 8 (over z, y), sub: 4 (over x, core).
Axes of the slice: x: 2, y: 2, z: 4, core: 2. Of those that a mesh axis runs over, the one named last changes fastest.
Arguments:
- fine_latent: bfloat16 [1024, 64, 128], P(('dom', 'sub')), may hold values from -6 to 6
- coarse_latent: bfloat16 [256, 64, 128], P(('dom', 'sub')), may hold values from -6 to 6
- adj_index: int32 [1024, 16], P(('dom', 'sub')), may hold values from 0 to 63
- adj_weight: bfloat16 [1024, 64, 1024], P(('dom', 'sub')), may hold values from -0.1875 to 0.1875
- interp_slot: int32 [1024, 4], P(('dom', 'sub')), may hold values from 0 to 31
- interp_weight: bfloat16 [1024, 64, 256], P(('dom', 'sub')), may hold values from -0.375 to 0.375
- coarse_send: int32 [32, 32, 1], P(('dom', 'sub')), may hold values from 0 to 7
- halo_sub_send: int32 [32, 4, 4], P(('dom', 'sub')), may hold values from 0 to 31
- halo_dom_send: int32 [32, 2, 8], P(('dom', 'sub')), may hold values from 0 to 31
- block_count: int32 [32], P(('dom', 'sub')), may hold values from 16 to 32, as said below
- w_in: bfloat16 [2, 384, 128], replicated, may hold values from -0.3125 to 0.3125
- b_in: float32 [2, 128], replicated, may hold values from -3 to 3
- w_out: bfloat16 [2, 128, 128], replicated, may hold values from -0.5 to 0.5
- ln_gain: float32 [2, 128], replicated, may hold values from 0.25 to 1.75
Outputs:
- fine_out: bfloat16 [1024, 64, 128], P(('dom', 'sub'))
Inputs may be any that keep to these rules, and one draw needn't show every extreme that they name: `block_count`: some device has all 32 blocks live and some has half of them.
All inputs are finite; a program needn't handle non-finite values.
Results may differ from a plain program's by a relative error of at most 0.0058.
Values may be sent and summed in bfloat16 or wider, within the bound.
A program may use at most 64 MiB of HBM per device.

v0:
```python
import functools
import math

import jax
import jax.numpy as jnp
from jax import lax
from jax.experimental import pallas as pl
from jax.experimental.pallas import tpu as pltpu
from jax.sharding import PartitionSpec as P

MESH = pl.DeviceIdType.MESH


def kernel(
    n_dom,
    n_sub,
    steps,
    adj_index,
    interp_slot,
    coarse_send,
    halo_sub_send,
    halo_dom_send,
    block_count,
    fine_hbm,
    coarse_hbm,
    adj_hbm,
    interp_hbm,
    w_in,
    b_in,
    w_out,
    ln_gain,
    out,
    *scratch,
):
    held = scratch[:steps]
    pools = scratch[steps : 2 * steps]
    sub_outs = scratch[2 * steps : 3 * steps]
    dom_outs = scratch[3 * steps : 4 * steps]
    (
        coarse,
        adj,
        iw,
        coarse_out,
        received,
        interp,
        summed,
        load_sem,
        c_send,
        c_recv,
        s_send,
        s_recv,
        d_send,
        d_recv,
    ) = scratch[4 * steps :]

    n = n_dom * n_sub
    dom, sub = lax.axis_index("dom"), lax.axis_index("sub")
    me = dom * n_sub + sub
    n_fine, rows, lat = out.shape
    slots = coarse_out.shape[1]
    hs = sub_outs[0].shape[1]
    hd = dom_outs[0].shape[1]
    k_a, k_i = adj_index.shape[1], interp_slot.shape[1]

    barrier = pltpu.get_barrier_semaphore()

    def greet(o, _):
        d = lax.rem(me + o, n)
        pl.semaphore_signal(
            barrier, inc=1, device_id=(d // n_sub, lax.rem(d, n_sub)), device_id_type=MESH
        )
        return 0

    lax.fori_loop(1, n, greet, 0)

    loads = [
        pltpu.make_async_copy(src, dst, load_sem.at[i])
        for i, (src, dst) in enumerate(
            [(fine_hbm, held[0]), (coarse_hbm, coarse), (adj_hbm, adj), (interp_hbm, iw)]
        )
    ]
    for copy in loads:
        copy.start()

    def gather_halo(t):
        for i in range(n_sub):
            for s in range(hs):
                sub_outs[t][i, s] = held[t][halo_sub_send[0, i, s]]
        for i in range(2):
            for s in range(hd):
                dom_outs[t][i, s] = held[t][halo_dom_send[0, i, s]]

    def sub_copy(t, peer, owner):
        return pltpu.make_async_remote_copy(
            src_ref=sub_outs[t].at[peer],
            dst_ref=pools[t].at[pl.ds(n_fine + owner * hs, hs)],
            send_sem=s_send.at[t, peer],
            recv_sem=s_recv.at[t, owner],
            device_id=(dom, peer),
            device_id_type=MESH,
        )

    def dom_copy(t, way):
        target = dom + 1 if way == 0 else dom - 1
        return pltpu.make_async_remote_copy(
            src_ref=dom_outs[t].at[way],
            dst_ref=pools[t].at[pl.ds(n_fine + n_sub * hs + way * hd, hd)],
            send_sem=d_send.at[t, way],
            recv_sem=d_recv.at[t, way],
            device_id=(target, sub),
            device_id_type=MESH,
        )

    def coarse_copy(peer, owner):
        return pltpu.make_async_remote_copy(
            src_ref=coarse_out.at[peer],
            dst_ref=received.at[pl.ds(owner * slots, slots)],
            send_sem=c_send.at[peer],
            recv_sem=c_recv.at[owner],
            device_id=(peer // n_sub, lax.rem(peer, n_sub)),
            device_id_type=MESH,
        )

    def start_halo(t):
        @pl.when(dom < n_dom - 1)
        def _():
            dom_copy(t, 0).start()

        @pl.when(dom > 0)
        def _():
            dom_copy(t, 1).start()

        for o in range(1, n_sub):
            sub_copy(t, lax.rem(sub + o, n_sub), sub).start()

    def local_pool(t):
        pools[t][pl.ds(n_fine + sub * hs, hs)] = sub_outs[t][sub]
        base = n_fine + n_sub * hs

        @pl.when(dom == 0)
        def _():
            pools[t][pl.ds(base, hd)] = jnp.zeros((hd, rows, lat), pools[t].dtype)

        @pl.when(dom == n_dom - 1)
        def _():
            pools[t][pl.ds(base + hd, hd)] = jnp.zeros((hd, rows, lat), pools[t].dtype)

    def wait_halo(t):
        for o in range(1, n_sub):
            owner = lax.rem(sub + o, n_sub)
            sub_copy(t, owner, owner).wait_recv()

        @pl.when(dom > 0)
        def _():
            dom_copy(t, 0).wait_recv()

        @pl.when(dom < n_dom - 1)
        def _():
            dom_copy(t, 1).wait_recv()

    def finish_halo_sends(t):
        for o in range(1, n_sub):
            sub_copy(t, lax.rem(sub + o, n_sub), sub).wait_send()

        @pl.when(dom < n_dom - 1)
        def _():
            dom_copy(t, 0).wait_send()

        @pl.when(dom > 0)
        def _():
            dom_copy(t, 1).wait_send()

    loads[0].wait()
    gather_halo(0)
    loads[1].wait()

    def gather_coarse(d, _):
        for s in range(slots):
            coarse_out[d, s] = coarse[coarse_send[0, d, s]]
        return 0

    lax.fori_loop(0, n, gather_coarse, 0)

    pl.semaphore_wait(barrier, n - 1)
    start_halo(0)

    def send_coarse(o, _):
        coarse_copy(lax.rem(me + o, n), me).start()
        return 0

    lax.fori_loop(1, n, send_coarse, 0)

    received[pl.ds(me * slots, slots)] = coarse_out[me]
    pools[0][pl.ds(0, n_fine)] = held[0][...]
    local_pool(0)

    group = math.gcd(n_fine, 4)

    def product(weights, table, index, tiles, into):
        def body(g, _):
            for u in range(group):
                b = g * group + u
                picked = jnp.concatenate([table[index[b, k]] for k in range(tiles)], axis=0)
                into[b] = jnp.dot(
                    weights[b], picked, preferred_element_type=jnp.float32
                ).astype(into.dtype)
            return 0

        lax.fori_loop(0, n_fine // group, body, 0)

    chunk = math.gcd(n_fine, 8)
    live = block_count[0]

    for t in range(steps):
        wait_halo(t)
        if t == 0:
            loads[2].wait()
        product(adj, pools[t], adj_index, k_a, summed)
        if t == 0:
            def take_coarse(o, _):
                owner = lax.rem(me + n - o, n)
                coarse_copy(owner, owner).wait_recv()
                return 0

            lax.fori_loop(1, n, take_coarse, 0)
            loads[3].wait()
            product(iw, received, interp_slot, k_i, interp)

        def update(c, _):
            at = pl.ds(c * chunk, chunk)
            h = held[t][at].reshape(chunk * rows, lat)
            joined = jnp.concatenate(
                [
                    h,
                    summed[at].reshape(chunk * rows, lat),
                    interp[at].reshape(chunk * rows, lat),
                ],
                axis=1,
            )
            hidden = jnp.dot(joined, w_in[t], preferred_element_type=jnp.float32)
            hidden = jnp.maximum(hidden + b_in[pl.ds(t, 1)], 0.0).astype(jnp.bfloat16)
            value = jnp.dot(hidden, w_out[t], preferred_element_type=jnp.float32)
            centred = value - jnp.mean(value, axis=-1, keepdims=True)
            variance = jnp.mean(centred * centred, axis=-1, keepdims=True)
            normed = centred * lax.rsqrt(variance + 1e-05) * ln_gain[pl.ds(t, 1)]
            updated = (h.astype(jnp.float32) + normed).reshape(chunk, rows, lat)
            block = c * chunk + lax.broadcasted_iota(jnp.int32, (chunk, rows, lat), 0)
            updated = jnp.where(block < live, updated, 0.0).astype(out.dtype)
            if t == steps - 1:
                out[at] = updated
            else:
                held[t + 1][at] = updated
                pools[t + 1][at] = updated
            return 0

        lax.fori_loop(0, n_fine // chunk, update, 0)
        if t < steps - 1:
            gather_halo(t + 1)
            start_halo(t + 1)
            local_pool(t + 1)

    for t in range(steps):
        finish_halo_sends(t)

    def sent_coarse(o, _):
        coarse_copy(lax.rem(me + o, n), me).wait_send()
        return 0

    lax.fori_loop(1, n, sent_coarse, 0)


def per_device(
    n_dom,
    n_sub,
    fine_latent,
    coarse_latent,
    adj_index,
    adj_weight,
    interp_slot,
    interp_weight,
    coarse_send,
    halo_sub_send,
    halo_dom_send,
    block_count,
    w_in,
    b_in,
    w_out,
    ln_gain,
):
    n = n_dom * n_sub
    steps = w_in.shape[0]
    n_fine, rows, lat = fine_latent.shape
    slots = coarse_send.shape[2]
    hs, hd = halo_sub_send.shape[2], halo_dom_send.shape[2]
    pool = n_fine + n_sub * hs + 2 * hd
    kind = fine_latent.dtype

    def vmem(*lead):
        return pltpu.VMEM(lead + (rows, lat), kind)

    dma = pltpu.SemaphoreType.DMA
    scratch = (
        [vmem(n_fine)] * steps
        + [vmem(pool)] * steps
        + [vmem(n_sub, hs)] * steps
        + [vmem(2, hd)] * steps
        + [
            pltpu.VMEM(coarse_latent.shape, kind),
            pltpu.VMEM(adj_weight.shape, kind),
            pltpu.VMEM(interp_weight.shape, kind),
            vmem(n, slots),
            vmem(n * slots),
            vmem(n_fine),
            vmem(n_fine),
            dma((4,)),
            dma((n,)),
            dma((n,)),
            dma((steps, n_sub)),
            dma((steps, n_sub)),
            dma((steps, 2)),
            dma((steps, 2)),
        ]
    )
    smem = pl.BlockSpec(memory_space=pltpu.SMEM)
    hbm = pl.BlockSpec(memory_space=pl.ANY)
    whole = pl.BlockSpec(memory_space=pltpu.VMEM)
    return pl.pallas_call(
        functools.partial(kernel, n_dom, n_sub, steps),
        out_shape=jax.ShapeDtypeStruct(fine_latent.shape, kind),
        in_specs=[smem] * 6 + [hbm] * 4 + [whole] * 4,
        out_specs=whole,
        scratch_shapes=scratch,
        compiler_params=pltpu.CompilerParams(
            collective_id=0, has_side_effects=True, vmem_limit_bytes=48 * 1024 * 1024
        ),
        name="graph_steps",
    )(
        adj_index,
        interp_slot,
        coarse_send,
        halo_sub_send,
        halo_dom_send,
        block_count,
        fine_latent,
        coarse_latent,
        adj_weight,
        interp_weight,
        w_in,
        b_in,
        w_out,
        ln_gain,
    )


def solution(mesh):
    placed = (
        P(("dom", "sub"), None, None),
        P(("dom", "sub"), None, None),
        P(("dom", "sub"), None),
        P(("dom", "sub"), None, None),
        P(("dom", "sub"), None),
        P(("dom", "sub"), None, None),
        P(("dom", "sub"), None, None),
        P(("dom", "sub"), None, None),
        P(("dom", "sub"), None, None),
        P(("dom", "sub")),
        P(),
        P(),
        P(),
        P(),
    )
    return jax.shard_map(
        functools.partial(per_device, mesh.shape["dom"], mesh.shape["sub"]),
        mesh=mesh,
        in_specs=placed,
        out_specs=P(("dom", "sub"), None, None),
        check_vma=False,
    )
```

profile of v0, /device:TPU:9, one launch (start us, length us, event | category | flops | bytes accessed | tf_op | source)
XLA Modules:
  0.0 49.2 jit_solution(7467814344514175413)
XLA Ops:
  0.7 0.8 %copy.15.adj_index = s32[32,16]{1,0:T(8,128)S(1)} copy(s32[32,16]{0,1:T(8,128)} %param.16) | data formatting | bytes 4096 | tf_op args[2]
  1.4 0.8 %copy.16.interp_slot = s32[32,4]{1,0:T(8,128)S(1)} copy(s32[32,4]{0,1:T(4,128)} %param.18) | data formatting | bytes 1024 | tf_op args[4]
  2.2 0.7 %copy.17.coarse_send = s32[1,32,1]{2,1,0:T(8,128)S(1)} copy(s32[1,32,1]{1,2,0:T(1,128)} %param.20) | data formatting | bytes 256 | tf_op args[6]
  2.9 0.0 copy-start
  2.9 1.2 %copy-done = bf16[32,64,256]{2,1,0:T(8,128)(2,1)S(1)} copy-done((bf16[32,64,256]{2,1,0:T(8,128)(2,1)S(1)}, bf16[32,64,256]{2,1,0:T(8,128)(2,1)}, u32[]{:S(2)}) %copy-start) | copy-done | bytes 1048600
  4.1 0.0 copy-start.1
  4.2 1.0 %copy-done.1 = bf16[32,64,128]{2,1,0:T(8,128)(2,1)S(1)} copy-done((bf16[32,64,128]{2,1,0:T(8,128)(2,1)S(1)}, bf16[32,64,128]{2,1,0:T(8,128)(2,1)}, u32[]{:S(2)}) %copy-start.1) | copy-done | bytes 524312
  5.2 0.0 copy-start.2
  5.2 0.9 %copy-done.2 = bf16[2,384,128]{2,1,0:T(8,128)(2,1)S(1)} copy-done((bf16[2,384,128]{2,1,0:T(8,128)(2,1)S(1)}, bf16[2,384,128]{2,1,0:T(8,128)(2,1)}, u32[]{:S(2)}) %copy-start.2) | copy-done | bytes 196632
  6.1 0.0 copy-start.3
  6.1 0.9 %copy-done.3 = bf16[8,64,128]{2,1,0:T(8,128)(2,1)S(1)} copy-done((bf16[8,64,128]{2,1,0:T(8,128)(2,1)S(1)}, bf16[8,64,128]{2,1,0:T(8,128)(2,1)}, u32[]{:S(2)}) %copy-start.3) | copy-done | bytes 131096
  7.0 0.0 copy-start.4
  7.0 0.8 %copy-done.4 = bf16[2,128,128]{2,1,0:T(8,128)(2,1)S(1)} copy-done((bf16[2,128,128]{2,1,0:T(8,128)(2,1)S(1)}, bf16[2,128,128]{2,1,0:T(8,128)(2,1)}, u32[]{:S(2)}) %copy-start.4) | copy-done | bytes 65560
  7.9 0.0 copy-start.5
  7.9 0.7 %copy-done.5 = s32[1,4,4]{2,1,0:T(4,128)S(1)} copy-done((s32[1,4,4]{2,1,0:T(4,128)S(1)}, s32[1,4,4]{2,1,0:T(4,128)}, u32[]{:S(2)}) %copy-start.5) | copy-done | bytes 88
  8.5 0.0 copy-start.6
  8.5 0.7 %copy-done.6 = s32[1,2,8]{2,1,0:T(2,128)S(1)} copy-done((s32[1,2,8]{2,1,0:T(2,128)S(1)}, s32[1,2,8]{2,1,0:T(2,128)}, u32[]{:S(2)}) %copy-start.6) | copy-done | bytes 88
  9.2 0.0 copy-start.7
  9.2 0.7 %copy-done.7 = f32[2,128]{1,0:T(2,128)S(1)} copy-done((f32[2,128]{1,0:T(2,128)S(1)}, f32[2,128]{1,0:T(2,128)}, u32[]{:S(2)}) %copy-start.7) | copy-done | bytes 1048
  9.9 0.0 copy-start.8
  9.9 0.7 %copy-done.8 = f32[2,128]{1,0:T(2,128)S(1)} copy-done((f32[2,128]{1,0:T(2,128)S(1)}, f32[2,128]{1,0:T(2,128)}, u32[]{:S(2)}) %copy-start.8) | copy-done | bytes 1048
  10.6 37.9 %graph_steps.1 = bf16[32,64,128]{2,1,0:T(8,128)(2,1)S(1)} custom-call(s32[32,16]{1,0:T(8,128)S(1)} %copy.15.adj_index, s32[32,4]{1,0:T(8,128)S(1)} %copy.16.interp_slot, s32[1,32,1]{2,1,0:T(8,128)S(1)} %copy.17.coarse_send, s32[1,4,4]{2,1,0:T(4,128)S(1)} %copy-done.5, s32[1,2,8]{2,1,0:T(2,128)S(1)} %copy-done.6, s32[1]{0:T(128)S(6)} %copy.19.block_count, ...), custom_call_target="tpu_custom_call" | custom-call | tf_op jit(solution)/shard_map/graph_steps/pallas_call | solution.py:327
  48.5 0.8 %copy.20 = bf16[32,64,128]{2,1,0:T(8,128)(2,1)} copy(bf16[32,64,128]{2,1,0:T(8,128)(2,1)S(1)} %graph_steps.1) | data formatting | bytes 1048576
Async XLA Ops:
  2.9 1.2 %copy-start = (bf16[32,64,256]{2,1,0:T(8,128)(2,1)S(1)}, bf16[32,64,256]{2,1,0:T(8,128)(2,1)}, u32[]{:S(2)}) copy-start(bf16[32,64,256]{2,1,0:T(8,128)(2,1)} %interp_hbm.1) | copy-start | bytes 3145732
  4.1 1.0 %copy-start.1 = (bf16[32,64,128]{2,1,0:T(8,128)(2,1)S(1)}, bf16[32,64,128]{2,1,0:T(8,128)(2,1)}, u32[]{:S(2)}) copy-start(bf16[32,64,128]{2,1,0:T(8,128)(2,1)} %fine_hbm.1) | copy-start | bytes 1572868
  5.2 0.9 %copy-start.2 = (bf16[2,384,128]{2,1,0:T(8,128)(2,1)S(1)}, bf16[2,384,128]{2,1,0:T(8,128)(2,1)}, u32[]{:S(2)}) copy-start(bf16[2,384,128]{2,1,0:T(8,128)(2,1)} %w_in.1) | copy-start | bytes 589828
  6.1 0.9 %copy-start.3 = (bf16[8,64,128]{2,1,0:T(8,128)(2,1)S(1)}, bf16[8,64,128]{2,1,0:T(8,128)(2,1)}, u32[]{:S(2)}) copy-start(bf16[8,64,128]{2,1,0:T(8,128)(2,1)} %coarse_hbm.1) | copy-start | bytes 393220
  7.0 0.8 %copy-start.4 = (bf16[2,128,128]{2,1,0:T(8,128)(2,1)S(1)}, bf16[2,128,128]{2,1,0:T(8,128)(2,1)}, u32[]{:S(2)}) copy-start(bf16[2,128,128]{2,1,0:T(8,128)(2,1)} %w_out.1) | copy-start | bytes 196612
  7.9 0.7 %copy-start.5 = (s32[1,4,4]{2,1,0:T(4,128)S(1)}, s32[1,4,4]{2,1,0:T(4,128)}, u32[]{:S(2)}) copy-start(s32[1,4,4]{2,1,0:T(4,128)} %halo_sub_send.1) | copy-start | bytes 196
  8.5 0.7 %copy-start.6 = (s32[1,2,8]{2,1,0:T(2,128)S(1)}, s32[1,2,8]{2,1,0:T(2,128)}, u32[]{:S(2)}) copy-start(s32[1,2,8]{2,1,0:T(2,128)} %halo_dom_send.1) | copy-start | bytes 196
  9.2 0.7 %copy-start.7 = (f32[2,128]{1,0:T(2,128)S(1)}, f32[2,128]{1,0:T(2,128)}, u32[]{:S(2)}) copy-start(f32[2,128]{1,0:T(2,128)} %b_in.1) | copy-start | bytes 3076
  9.9 0.7 %copy-start.8 = (f32[2,128]{1,0:T(2,128)S(1)}, f32[2,128]{1,0:T(2,128)}, u32[]{:S(2)}) copy-start(f32[2,128]{1,0:T(2,128)} %ln_gain.1) | copy-start | bytes 3076
where the time goes:
time: 50.2 us; the launch traced here: 49.2 us
  Pallas kernels  37.9 us (75%)
  local copies, waits for them, and re-layouts  10.7 us (21%)
  between operations  0.67 us (1%)
    pallas_call x1, Pallas kernels, per_device(): pl.pallas_call(functools.partial(kernel, n_dom, n_sub, steps), out_shape=...  37.9 us
    unnamed x22, local copies, waits for them, and re-layouts  10.7 us

commit v1 on v0

--- a/solution.py
+++ b/solution.py
@@ -60,7 +60,7 @@
     slots = coarse_out.shape[1]
     hs = sub_outs[0].shape[1]
     hd = dom_outs[0].shape[1]
-    k_a, k_i = adj_index.shape[1], interp_slot.shape[1]
+    k_a, k_i = adj_index.shape[0], interp_slot.shape[0]
 
     barrier = pltpu.get_barrier_semaphore()
 
@@ -176,7 +176,7 @@
 
     def gather_coarse(d, _):
         for s in range(slots):
-            coarse_out[d, s] = coarse[coarse_send[0, d, s]]
+            coarse_out[d, s] = coarse[coarse_send[0, s, d]]
         return 0
 
     lax.fori_loop(0, n, gather_coarse, 0)
@@ -200,7 +200,7 @@
         def body(g, _):
             for u in range(group):
                 b = g * group + u
-                picked = jnp.concatenate([table[index[b, k]] for k in range(tiles)], axis=0)
+                picked = jnp.concatenate([table[index[k, b]] for k in range(tiles)], axis=0)
                 into[b] = jnp.dot(
                     weights[b], picked, preferred_element_type=jnp.float32
                 ).astype(into.dtype)
@@ -209,7 +209,7 @@
         lax.fori_loop(0, n_fine // group, body, 0)
 
     chunk = math.gcd(n_fine, 8)
-    live = block_count[0]
+    live = block_count[0, 0]
 
     for t in range(steps):
         wait_halo(t)
@@ -331,16 +331,16 @@
         out_specs=whole,
         scratch_shapes=scratch,
         compiler_params=pltpu.CompilerParams(
-            collective_id=0, has_side_effects=True, vmem_limit_bytes=48 * 1024 * 1024
+            collective_id=0, has_side_effects=True, vmem_limit_bytes=67043328
         ),
         name="graph_steps",
     )(
-        adj_index,
-        interp_slot,
-        coarse_send,
+        adj_index.T,
+        interp_slot.T,
+        coarse_send.transpose(0, 2, 1),
         halo_sub_send,
         halo_dom_send,
-        block_count,
+        block_count.reshape(1, 1),
         fine_latent,
         coarse_latent,
         adj_weight,

time: 50.2 us -> 41.5 us (0.83)
  local copies, waits for them, and re-layouts: 10.7 us -> 1.87 us
    unnamed x22 -> x1, local copies, waits for them, and re-layouts: 10.7 us -> 1.87 us
where the time goes in v1:
time: 41.5 us; the launch traced here: 40.8 us
  Pallas kernels  38.3 us (92%)
  local copies, waits for them, and re-layouts  1.87 us (5%)
  between operations  0.66 us (2%)
    pallas_call x1, Pallas kernels, per_device(): pl.pallas_call(functools.partial(kernel, n_dom, n_sub, steps), out_shape=...  38.3 us
    unnamed x1, local copies, waits for them, and re-layouts  1.87 us

profile of v1, /device:TPU:9, one launch (start us, length us, event | category | flops | bytes accessed | tf_op | source)
XLA Modules:
  0.0 40.8 jit_solution(12917880791706050175)
XLA Ops:
  0.7 38.3 %graph_steps.1 = bf16[32,64,128]{2,1,0:T(8,128)(2,1)} custom-call(s32[16,32]{1,0:T(8,128)} %bitcast.5, s32[4,32]{1,0:T(4,128)} %bitcast.6, s32[1,1,32]{2,1,0:T(1,128)} %bitcast.7, s32[1,4,4]{2,1,0:T(4,128)} %halo_sub_send.1, s32[1,2,8]{2,1,0:T(2,128)} %halo_dom_send.1, s32[1,1]{1,0:T(1,128)} %bitcast.4.block_count, bf16[32,64,128]{2,1,0:T(8,128)(2,1)} %fine_hbm.1, ...), custom_call_target="tpu_custom_call" | custom-call | tf_op jit(solution)/shard_map/graph_steps/pallas_call | solution.py:327
  39.0 1.9 %copy.17 = bf16[32,64,128]{2,1,0:T(8,128)(2,1)} copy(bf16[32,64,128]{2,1,0:T(8,128)(2,1)} %graph_steps.1) | data formatting | bytes 1048576

commit v2 on v1

--- a/solution.py
+++ b/solution.py
@@ -25,11 +25,11 @@
     coarse_hbm,
     adj_hbm,
     interp_hbm,
-    w_in,
-    b_in,
-    w_out,
-    ln_gain,
-    out,
+    w_in_hbm,
+    b_in_hbm,
+    w_out_hbm,
+    ln_gain_hbm,
+    out_hbm,
     *scratch,
 ):
     held = scratch[:steps]
@@ -44,7 +44,13 @@
         received,
         interp,
         summed,
+        w_in,
+        b_in,
+        w_out,
+        ln_gain,
         load_sem,
+        out,
+        out_sem,
         c_send,
         c_recv,
         s_send,
@@ -56,7 +62,7 @@
     n = n_dom * n_sub
     dom, sub = lax.axis_index("dom"), lax.axis_index("sub")
     me = dom * n_sub + sub
-    n_fine, rows, lat = out.shape
+    n_fine, rows, lat = out_hbm.shape
     slots = coarse_out.shape[1]
     hs = sub_outs[0].shape[1]
     hd = dom_outs[0].shape[1]
@@ -64,19 +70,36 @@
 
     barrier = pltpu.get_barrier_semaphore()
 
-    def greet(o, _):
-        d = lax.rem(me + o, n)
-        pl.semaphore_signal(
-            barrier, inc=1, device_id=(d // n_sub, lax.rem(d, n_sub)), device_id_type=MESH
-        )
-        return 0
-
-    lax.fori_loop(1, n, greet, 0)
+    def wrapped(position, size):
+        return jnp.where(position >= size, position - size, position)
+
+    subs = [wrapped(sub + o, n_sub) for o in range(n_sub)]
+    ways = sorted(range(1, n_dom), key=lambda o: abs(o - n_dom // 2))
+
+    def peers(act):
+        for o in ways + [0]:
+            to = wrapped(dom + o, n_dom)
+            for other in subs[1:] if o == 0 else subs:
+                act(to, other)
+
+    def greet(to, other):
+        pl.semaphore_signal(barrier, inc=1, device_id=(to, other), device_id_type=MESH)
+
+    peers(greet)
 
     loads = [
         pltpu.make_async_copy(src, dst, load_sem.at[i])
         for i, (src, dst) in enumerate(
-            [(fine_hbm, held[0]), (coarse_hbm, coarse), (adj_hbm, adj), (interp_hbm, iw)]
+            [
+                (fine_hbm, held[0]),
+                (coarse_hbm, coarse),
+                (adj_hbm, adj),
+                (interp_hbm, iw),
+                (w_in_hbm, w_in),
+                (b_in_hbm, b_in),
+                (w_out_hbm, w_out),
+                (ln_gain_hbm, ln_gain),
+            ]
         )
     ]
     for copy in loads:
@@ -111,13 +134,14 @@
             device_id_type=MESH,
         )
 
-    def coarse_copy(peer, owner):
+    def coarse_copy(to, other, owner):
+        peer = to * n_sub + other
         return pltpu.make_async_remote_copy(
             src_ref=coarse_out.at[peer],
             dst_ref=received.at[pl.ds(owner * slots, slots)],
             send_sem=c_send.at[peer],
             recv_sem=c_recv.at[owner],
-            device_id=(peer // n_sub, lax.rem(peer, n_sub)),
+            device_id=(to, other),
             device_id_type=MESH,
         )
 
@@ -131,7 +155,7 @@
             dom_copy(t, 1).start()
 
         for o in range(1, n_sub):
-            sub_copy(t, lax.rem(sub + o, n_sub), sub).start()
+            sub_copy(t, subs[o], sub).start()
 
     def local_pool(t):
         pools[t][pl.ds(n_fine + sub * hs, hs)] = sub_outs[t][sub]
@@ -147,7 +171,7 @@
 
     def wait_halo(t):
         for o in range(1, n_sub):
-            owner = lax.rem(sub + o, n_sub)
+            owner = subs[o]
             sub_copy(t, owner, owner).wait_recv()
 
         @pl.when(dom > 0)
@@ -160,7 +184,7 @@
 
     def finish_halo_sends(t):
         for o in range(1, n_sub):
-            sub_copy(t, lax.rem(sub + o, n_sub), sub).wait_send()
+            sub_copy(t, subs[o], sub).wait_send()
 
         @pl.when(dom < n_dom - 1)
         def _():
@@ -184,11 +208,7 @@
     pl.semaphore_wait(barrier, n - 1)
     start_halo(0)
 
-    def send_coarse(o, _):
-        coarse_copy(lax.rem(me + o, n), me).start()
-        return 0
-
-    lax.fori_loop(1, n, send_coarse, 0)
+    peers(lambda to, other: coarse_copy(to, other, me).start())
 
     received[pl.ds(me * slots, slots)] = coarse_out[me]
     pools[0][pl.ds(0, n_fine)] = held[0][...]
@@ -211,19 +231,19 @@
     chunk = math.gcd(n_fine, 8)
     live = block_count[0, 0]
 
+    def stored(c):
+        at = pl.ds(c * chunk, chunk)
+        return pltpu.make_async_copy(out.at[at], out_hbm.at[at], out_sem.at[c])
+
     for t in range(steps):
         wait_halo(t)
         if t == 0:
             loads[2].wait()
         product(adj, pools[t], adj_index, k_a, summed)
         if t == 0:
-            def take_coarse(o, _):
-                owner = lax.rem(me + n - o, n)
-                coarse_copy(owner, owner).wait_recv()
-                return 0
-
-            lax.fori_loop(1, n, take_coarse, 0)
-            loads[3].wait()
+            peers(lambda to, other: coarse_copy(to, other, to * n_sub + other).wait_recv())
+            for copy in loads[3:]:
+                copy.wait()
             product(iw, received, interp_slot, k_i, interp)
 
         def update(c, _):
@@ -248,6 +268,7 @@
             updated = jnp.where(block < live, updated, 0.0).astype(out.dtype)
             if t == steps - 1:
                 out[at] = updated
+                stored(c).start()
             else:
                 held[t + 1][at] = updated
                 pools[t + 1][at] = updated
@@ -261,12 +282,10 @@
 
     for t in range(steps):
         finish_halo_sends(t)
-
-    def sent_coarse(o, _):
-        coarse_copy(lax.rem(me + o, n), me).wait_send()
-        return 0
-
-    lax.fori_loop(1, n, sent_coarse, 0)
+    for c in range(n_fine // chunk):
+        stored(c).wait()
+
+    peers(lambda to, other: coarse_copy(to, other, me).wait_send())
 
 
 def per_device(
@@ -312,7 +331,13 @@
             vmem(n * slots),
             vmem(n_fine),
             vmem(n_fine),
-            dma((4,)),
+            pltpu.VMEM(w_in.shape, w_in.dtype),
+            pltpu.VMEM(b_in.shape, b_in.dtype),
+            pltpu.VMEM(w_out.shape, w_out.dtype),
+            pltpu.VMEM(ln_gain.shape, ln_gain.dtype),
+            dma((8,)),
+            vmem(n_fine),
+            dma((n_fine,)),
             dma((n,)),
             dma((n,)),
             dma((steps, n_sub)),
@@ -323,12 +348,11 @@
     )
     smem = pl.BlockSpec(memory_space=pltpu.SMEM)
     hbm = pl.BlockSpec(memory_space=pl.ANY)
-    whole = pl.BlockSpec(memory_space=pltpu.VMEM)
     return pl.pallas_call(
         functools.partial(kernel, n_dom, n_sub, steps),
         out_shape=jax.ShapeDtypeStruct(fine_latent.shape, kind),
-        in_specs=[smem] * 6 + [hbm] * 4 + [whole] * 4,
-        out_specs=whole,
+        in_specs=[smem] * 6 + [hbm] * 8,
+        out_specs=hbm,
         scratch_shapes=scratch,
         compiler_params=pltpu.CompilerParams(
             collective_id=0, has_side_effects=True, vmem_limit_bytes=67043328

time: 41.5 us -> 41.1 us (level); the launches traced: 40.8 us -> 40.9 us
  no operation moved by 1% of the time
where the time goes in v2:
time: 41.1 us; the launch traced here: 40.9 us
  Pallas kernels  38.3 us (93%)
  local copies, waits for them, and re-layouts  1.87 us (5%)
  between operations  0.66 us (2%)
    pallas_call x1, Pallas kernels, per_device(): pl.pallas_call(functools.partial(kernel, n_dom, n_sub, steps), out_shape=...  38.3 us
    unnamed x1, local copies, waits for them, and re-layouts  1.87 us

profile of v2, /device:TPU:9, one launch (start us, length us, event | category | flops | bytes accessed | tf_op | source)
XLA Modules:
  0.0 40.9 jit_solution(14307022224313875296)
XLA Ops:
  0.7 38.3 %graph_steps.1 = bf16[32,64,128]{2,1,0:T(8,128)(2,1)} custom-call(s32[16,32]{1,0:T(8,128)} %bitcast.5, s32[4,32]{1,0:T(4,128)} %bitcast.6, s32[1,1,32]{2,1,0:T(1,128)} %bitcast.7, s32[1,4,4]{2,1,0:T(4,128)} %halo_sub_send.1, s32[1,2,8]{2,1,0:T(2,128)} %halo_dom_send.1, s32[1,1]{1,0:T(1,128)} %bitcast.4.block_count, bf16[32,64,128]{2,1,0:T(8,128)(2,1)} %fine_hbm.1, ...), custom_call_target="tpu_custom_call" | custom-call | tf_op jit(solution)/shard_map/graph_steps/pallas_call | solution.py:351
  39.0 1.9 %copy.17 = bf16[32,64,128]{2,1,0:T(8,128)(2,1)} copy(bf16[32,64,128]{2,1,0:T(8,128)(2,1)} %graph_steps.1) | data formatting | bytes 1048576

commit v3 on v2

--- a/solution.py
+++ b/solution.py
@@ -246,6 +246,13 @@
                 copy.wait()
             product(iw, received, interp_slot, k_i, interp)
 
+        wide = w_out[t].astype(jnp.float32)
+        wide = wide - jnp.mean(wide, axis=-1, keepdims=True)
+        high = wide.astype(jnp.bfloat16)
+        low = (wide - high.astype(jnp.float32)).astype(jnp.bfloat16)
+        split = jnp.concatenate([high, low], axis=1)
+        ones = jnp.ones((lat, lat), jnp.bfloat16)
+
         def update(c, _):
             at = pl.ds(c * chunk, chunk)
             h = held[t][at].reshape(chunk * rows, lat)
@@ -259,9 +266,10 @@
             )
             hidden = jnp.dot(joined, w_in[t], preferred_element_type=jnp.float32)
             hidden = jnp.maximum(hidden + b_in[pl.ds(t, 1)], 0.0).astype(jnp.bfloat16)
-            value = jnp.dot(hidden, w_out[t], preferred_element_type=jnp.float32)
-            centred = value - jnp.mean(value, axis=-1, keepdims=True)
-            variance = jnp.mean(centred * centred, axis=-1, keepdims=True)
+            halves = jnp.dot(hidden, split, preferred_element_type=jnp.float32)
+            centred = halves[:, :lat] + halves[:, lat:]
+            squares = (centred * centred).astype(jnp.bfloat16)
+            variance = jnp.dot(squares, ones, preferred_element_type=jnp.float32) * (1.0 / lat)
             normed = centred * lax.rsqrt(variance + 1e-05) * ln_gain[pl.ds(t, 1)]
             updated = (h.astype(jnp.float32) + normed).reshape(chunk, rows, lat)
             block = c * chunk + lax.broadcasted_iota(jnp.int32, (chunk, rows, lat), 0)

time: 41.1 us -> 40.9 us (level)
  no operation moved by 1% of the time
where the time goes in v3:
time: 40.9 us; the launch traced here: 40.7 us
  Pallas kernels  38.2 us (93%)
  local copies, waits for them, and re-layouts  1.87 us (5%)
  between operations  0.66 us (2%)
    pallas_call x1, Pallas kernels, per_device(): pl.pallas_call(functools.partial(kernel, n_dom, n_sub, steps), out_shape=...  38.2 us
    unnamed x1, local copies, waits for them, and re-layouts  1.87 us

profile of v3, /device:TPU:9, one launch (start us, length us, event | category | flops | bytes accessed | tf_op | source)
XLA Modules:
  0.0 40.7 jit_solution(1621232773511095806)
XLA Ops:
  0.7 38.2 %graph_steps.1 = bf16[32,64,128]{2,1,0:T(8,128)(2,1)} custom-call(s32[16,32]{1,0:T(8,128)} %bitcast.5, s32[4,32]{1,0:T(4,128)} %bitcast.6, s32[1,1,32]{2,1,0:T(1,128)} %bitcast.7, s32[1,4,4]{2,1,0:T(4,128)} %halo_sub_send.1, s32[1,2,8]{2,1,0:T(2,128)} %halo_dom_send.1, s32[1,1]{1,0:T(1,128)} %bitcast.4.block_count, bf16[32,64,128]{2,1,0:T(8,128)(2,1)} %fine_hbm.1, ...), custom_call_target="tpu_custom_call" | custom-call | tf_op jit(solution)/shard_map/graph_steps/pallas_call | solution.py:359
  38.9 1.9 %copy.17 = bf16[32,64,128]{2,1,0:T(8,128)(2,1)} copy(bf16[32,64,128]{2,1,0:T(8,128)(2,1)} %graph_steps.1) | data formatting | bytes 1048576

commit v4 on v3

--- a/solution.py
+++ b/solution.py
@@ -105,10 +105,12 @@
     for copy in loads:
         copy.start()
 
-    def gather_halo(t):
+    def gather_sub(t):
         for i in range(n_sub):
             for s in range(hs):
                 sub_outs[t][i, s] = held[t][halo_sub_send[0, i, s]]
+
+    def gather_dom(t):
         for i in range(2):
             for s in range(hd):
                 dom_outs[t][i, s] = held[t][halo_dom_send[0, i, s]]
@@ -145,7 +147,7 @@
             device_id_type=MESH,
         )
 
-    def start_halo(t):
+    def start_dom(t):
         @pl.when(dom < n_dom - 1)
         def _():
             dom_copy(t, 0).start()
@@ -154,6 +156,7 @@
         def _():
             dom_copy(t, 1).start()
 
+    def start_sub(t):
         for o in range(1, n_sub):
             sub_copy(t, subs[o], sub).start()
 
@@ -195,7 +198,8 @@
             dom_copy(t, 1).wait_send()
 
     loads[0].wait()
-    gather_halo(0)
+    gather_dom(0)
+    gather_sub(0)
     loads[1].wait()
 
     def gather_coarse(d, _):
@@ -206,7 +210,8 @@
     lax.fori_loop(0, n, gather_coarse, 0)
 
     pl.semaphore_wait(barrier, n - 1)
-    start_halo(0)
+    start_dom(0)
+    start_sub(0)
 
     peers(lambda to, other: coarse_copy(to, other, me).start())
 
@@ -214,7 +219,7 @@
     pools[0][pl.ds(0, n_fine)] = held[0][...]
     local_pool(0)
 
-    group = math.gcd(n_fine, 4)
+    group = math.gcd(n_fine, 16)
 
     def product(weights, table, index, tiles, into):
         def body(g, _):
@@ -228,7 +233,7 @@
 
         lax.fori_loop(0, n_fine // group, body, 0)
 
-    chunk = math.gcd(n_fine, 8)
+    chunk = math.gcd(n_fine, 32)
     live = block_count[0, 0]
 
     def stored(c):
@@ -284,8 +289,10 @@
 
         lax.fori_loop(0, n_fine // chunk, update, 0)
         if t < steps - 1:
-            gather_halo(t + 1)
-            start_halo(t + 1)
+            gather_dom(t + 1)
+            start_dom(t + 1)
+            gather_sub(t + 1)
+            start_sub(t + 1)
             local_pool(t + 1)
 
     for t in range(steps):

time: 40.9 us -> 36.9 us (0.902)
  Pallas kernels: 38.2 us -> 34.1 us
    pallas_call x1, Pallas kernels: 38.2 us -> 34.1 us  [per_device(): pl.pallas_call(functools.partial(kernel, n_dom, n_sub, steps), out_shape=...]
where the time goes in v4:
time: 36.9 us; the launch traced here: 36.6 us
  Pallas kernels  34.1 us (92%)
  local copies, waits for them, and re-layouts  1.87 us (5%)
  between operations  0.66 us (2%)
    pallas_call x1, Pallas kernels, per_device(): pl.pallas_call(functools.partial(kernel, n_dom, n_sub, steps), out_shape=...  34.1 us
    unnamed x1, local copies, waits for them, and re-layouts  1.87 us

profile of v4, /device:TPU:9, one launch (start us, length us, event | category | flops | bytes accessed | tf_op | source)
XLA Modules:
  0.0 36.6 jit_solution(2075730201975874253)
XLA Ops:
  0.7 34.1 %graph_steps.1 = bf16[32,64,128]{2,1,0:T(8,128)(2,1)} custom-call(s32[16,32]{1,0:T(8,128)} %bitcast.5, s32[4,32]{1,0:T(4,128)} %bitcast.6, s32[1,1,32]{2,1,0:T(1,128)} %bitcast.7, s32[1,4,4]{2,1,0:T(4,128)} %halo_sub_send.1, s32[1,2,8]{2,1,0:T(2,128)} %halo_dom_send.1, s32[1,1]{1,0:T(1,128)} %bitcast.4.block_count, bf16[32,64,128]{2,1,0:T(8,128)(2,1)} %fine_hbm.1, ...), custom_call_target="tpu_custom_call" | custom-call | tf_op jit(solution)/shard_map/graph_steps/pallas_call | solution.py:366
  34.8 1.9 %copy.17 = bf16[32,64,128]{2,1,0:T(8,128)(2,1)} copy(bf16[32,64,128]{2,1,0:T(8,128)(2,1)} %graph_steps.1) | data formatting | bytes 1048576
